TPU v7x, 256 devices: a whole 4x4x8 slice. The times are simulated.
256 devices in a mesh: dom: 64 (over y, z_lo, x, core), rep: 4 (over z_hi).
Axes of the slice: x: 4, y: 4, z: 8 (z_hi: 4, z_lo: 2; z = z_hi * 2 + z_lo), core: 2. Of those that a mesh axis runs over, the one named last changes fastest.
Arguments:
- entities: float32 [16384, 512], P('dom'), may hold values from -1.5 to 1.5
- ent_accum: float32 [16384], P('dom'), may hold values from 0.5 to 20
- relations: float32 [8, 512, 512], P('rep'), may hold values from -0.25 to 0.25
- rel_accum: float32 [8, 512, 512], P('rep'), may hold values from 29.4912 to 294.912
- heads: int32 [3, 196608], P(None, ('dom', 'rep')), may hold values from 0 to 255
- tails: int32 [3, 196608], P(None, ('dom', 'rep')), may hold values from 0 to 255
- relation_ids: int32 [3, 196608], P(None, ('dom', 'rep')), may hold values from 0 to 1
- negatives: int32 [3, 65536], P(None, ('dom', 'rep')), may hold values from 0 to 255
Outputs:
- new_entities: float32 [16384, 512], P('dom')
- new_ent_accum: float32 [16384], P('dom')
- new_relations: float32 [8, 512, 512], P('rep')
- new_rel_accum: float32 [8, 512, 512], P('rep')
Inputs may be any that keep to these rules, and one draw needn't show every extreme that they name: `negatives`: rows within the named partition; some rows are named far more often than others.
All inputs are finite; a program needn't handle non-finite values.
Results may differ from a plain program's by a relative error of at most 0.0077.
Values may be sent and summed in bfloat16 or wider, within the bound.
No kernel may reach another device: no remote copies, remote signals or barrier semaphores. Data moves between devices by JAX's collectives and lax.ppermute only.
A program may use at most 64 MiB of HBM per device.

v0:
```python
import jax
import jax.numpy as jnp
from jax import lax
from jax.sharding import PartitionSpec as P

NCAP = 4
ROUNDS = 3


negative_weight = 0.0625
entity_rate = 0.05
relation_rate = 0.02


def from_behind(block, axis, distance):
    devices = range(lax.axis_size(axis))
    route = [((i - distance) % len(devices), i) for i in devices]
    return lax.ppermute(block, axis, route)


def bucket_terms(head_rows, tail_rows, neg_rows, rel_cat, rel_back, rel_ids):
    edges = head_rows.shape[0]
    width = head_rows.shape[1]
    kinds = rel_cat.shape[1] // width
    picks = (rel_ids[:, None] == jnp.arange(kinds, dtype=jnp.int32)[None, :]).astype(jnp.float32)
    proj = jnp.dot(head_rows, rel_cat, preferred_element_type=jnp.float32).reshape(
        edges, kinds, width
    )
    query = jnp.sum(proj * picks[:, :, None], axis=1).astype(jnp.bfloat16)
    columns = jnp.concatenate([tail_rows, neg_rows], axis=0)
    scores = lax.dot_general(
        query, columns, (((1,), (1,)), ((), ())), preferred_element_type=jnp.float32
    )
    diagonal = (
        jnp.arange(edges, dtype=jnp.int32)[:, None]
        == jnp.arange(columns.shape[0], dtype=jnp.int32)[None, :]
    )
    probs = jax.nn.sigmoid(scores)
    dscore = jnp.where(diagonal, probs - 1.0, negative_weight * probs).astype(jnp.bfloat16)
    dquery = jnp.dot(dscore, columns, preferred_element_type=jnp.float32).astype(jnp.bfloat16)
    dcolumns = lax.dot_general(
        dscore, query, (((0,), (0,)), ((), ())), preferred_element_type=jnp.float32
    )
    dhead_all = jnp.dot(dquery, rel_back, preferred_element_type=jnp.float32).reshape(
        edges, kinds, width
    )
    dhead = jnp.sum(dhead_all * picks[:, :, None], axis=1)
    masked = (head_rows[:, None, :] * picks[:, :, None].astype(head_rows.dtype)).reshape(
        edges, kinds * width
    )
    drel = lax.dot_general(
        masked, dquery, (((0,), (0,)), ((), ())), preferred_element_type=jnp.float32
    )
    return (dhead, dcolumns[:edges], dcolumns[edges:], drel.reshape(kinds, width, width))


def row_adagrad(param, accum, grads):
    accum = accum + jnp.mean(grads * grads, axis=-1)
    return (param - entity_rate * grads / jnp.sqrt(accum)[:, None], accum)


def full_adagrad(param, accum, grads):
    accum = accum + grads * grads
    return (param - relation_rate * grads / jnp.sqrt(accum), accum)


def on_device(entities, ent_accum, relations, rel_accum, heads, tails, relation_ids, negatives):
    rows, width = entities.shape
    parts = lax.axis_size("dom")
    rel_bf = relations.astype(jnp.bfloat16)
    kinds = rel_bf.shape[0]
    rel_cat = rel_bf.transpose(1, 0, 2).reshape(width, kinds * width)
    rel_back = rel_bf.transpose(2, 0, 1).reshape(width, kinds * width)
    rel_total = jnp.zeros((kinds, width, width), jnp.float32)
    for rnd in range(ROUNDS):
        offset = rnd + 1
        ent_bf = entities.astype(jnp.bfloat16)
        partner = from_behind(ent_bf, "dom", -offset)

        def fetch(wanted, table=ent_bf):
            taken = jnp.take(table, wanted, axis=0)
            return (lax.all_to_all(taken, "dom", split_axis=0, concat_axis=0, tiled=True), wanted)

        requests = negatives[rnd].reshape(parts, NCAP)
        neg_rows, served = fetch(
            lax.all_to_all(requests, "dom", split_axis=0, concat_axis=0, tiled=True)
        )
        head_idx = heads[rnd]
        tail_idx = tails[rnd]
        dhead, dtail, dneg, drel = bucket_terms(
            jnp.take(ent_bf, head_idx, axis=0),
            jnp.take(partner, tail_idx, axis=0),
            neg_rows.reshape(parts * NCAP, width),
            rel_cat,
            rel_back,
            relation_ids[rnd],
        )
        tail_block = jnp.zeros((rows, width), jnp.float32).at[tail_idx].add(dtail)
        returned = from_behind(tail_block, "dom", offset)
        neg_back = lax.all_to_all(
            dneg.reshape(parts, NCAP, width), "dom", split_axis=0, concat_axis=0, tiled=True
        )
        grads = returned.at[jnp.concatenate([head_idx, served.reshape(-1)])].add(
            jnp.concatenate([dhead, neg_back.reshape(parts * NCAP, width)], axis=0)
        )
        summed = lax.psum(grads, "rep")
        entities, ent_accum = row_adagrad(entities, ent_accum, summed)
        rel_total = rel_total + drel
    summed = lax.psum(rel_total, "dom")
    new_relations, new_rel_accum = full_adagrad(relations, rel_accum, summed)
    return (entities, ent_accum, new_relations, new_rel_accum)


def solution(mesh):
    in_specs = (
        P("dom", None),
        P("dom"),
        P("rep", None, None),
        P("rep", None, None),
        P(None, ("dom", "rep")),
        P(None, ("dom", "rep")),
        P(None, ("dom", "rep")),
        P(None, ("dom", "rep")),
    )
    out_specs = (P("dom", None), P("dom"), P("rep", None, None), P("rep", None, None))
    return jax.shard_map(
        on_device, mesh=mesh, in_specs=in_specs, out_specs=out_specs, check_vma=False
    )
```

profile of v0, /device:TPU:1, one launch (start us, length us, event | category | flops | bytes accessed | tf_op | source)
XLA Modules:
  0.0 1008.5 jit_solution(16201088587731078383)
XLA Ops:
  8.7 10.3 %all-to-all-start = ((s32[64,1,4]{2,1,0:T(1,128)}), s32[64,1,4]{2,1,0:T(1,128)S(1)}, u32[]{:S(2)}, u32[]{:S(2)}) async-start(s32[64,1,4]{2,1,0:T(1,128)} %bitcast.6), calls=%async_computation | async-start | bytes 65536 | tf_op jit(solution)/shard_map/all_to_all | solution.py:86
  24.8 2.7 gather_fusion
  27.5 1.4 copy.27
  29.1 3.5 multiply_reduce_fusion.5
  34.9 10.7 %all-to-all-start.1 = ((bf16[64,4,512]{2,1,0:T(4,128)(2,1)}), bf16[64,4,512]{2,1,0:T(4,128)(2,1)}, u32[]{:S(2)}, u32[]{:S(2)}) async-start(bf16[64,4,512]{2,1,0:T(4,128)(2,1)} %broadcast_select_fusion.8), calls=%async_computation.1 | async-start | bytes 524288 | tf_op jit(solution)/shard_map/all_to_all | solution.py:82
  47.0 2.3 copy.29
  49.2 2.7 gather_fusion.1
  53.0 2.3 all-to-all-done.1
  56.4 2.8 select_convert_fusion.2
  60.4 1.3 copy-done.10
  62.7 6.9 all-to-all-start.2
  71.7 8.2 scatter_custom_fusion
  79.8 1.6 collective-permute-start.1
  81.5 3.3 fusion.26
  84.8 8.1 all-to-all-start.3
  92.9 3.7 multiply_reduce_fusion.4
  96.9 9.4 scatter_custom_fusion.1
  106.4 54.9 %all-reduce.5.cloned.1.call-done = f32[256,512]{1,0:T(8,128)} async-done(((f32[256,512]{1,0:T(8,128)}), f32[256,512]{1,0:T(8,128)}) %all-reduce.5.cloned.1.call-update) | async-done | bytes 524304 | tf_op jit(solution)/shard_map/psum | solution.py:106
  161.4 1.2 multiply_reduce_fusion.8
  162.6 1.2 fusion.70
  163.7 6.0 collective-permute-start.2
  171.6 1.9 broadcast_select_fusion.7
  173.5 5.9 all-to-all-start.4
  179.4 3.3 gather_fusion.3
  182.7 1.3 broadcast_select_fusion.3
  184.0 3.5 multiply_reduce_fusion.3
  187.5 3.3 gather_fusion.4
  190.8 2.2 broadcast_select_fusion.2
  193.1 2.8 select_convert_fusion.1
  197.1 1.3 copy-done.9
  199.4 9.0 all-to-all-start.5
  209.3 8.2 scatter_custom_fusion.2
  217.5 1.5 collective-permute-start.3
  219.0 3.5 fusion.27
  222.5 8.7 all-to-all-start.6
  231.2 3.7 multiply_reduce_fusion.2
  235.9 9.3 scatter_custom_fusion.3
  245.4 51.5 %all-reduce.7.cloned.1.call-done = f32[256,512]{1,0:T(8,128)} async-done(((f32[256,512]{1,0:T(8,128)}), f32[256,512]{1,0:T(8,128)}) %all-reduce.7.cloned.1.call-update) | async-done | bytes 524304 | tf_op jit(solution)/shard_map/psum | solution.py:106
  297.0 1.2 multiply_reduce_fusion.7
  298.1 2.1 fusion.72
  300.2 6.9 collective-permute-start.4
  309.2 5.3 all-to-all-start.7
  314.5 2.7 gather_fusion.6
  317.4 3.5 multiply_reduce_fusion.1
  320.9 2.7 gather_fusion.7
  325.7 2.8 select_convert_fusion
  329.7 1.3 copy-done.8
  332.0 8.2 all-to-all-start.8
  340.3 1.2 copy.32
  342.3 3.7 fusion.21
  346.1 1.2 copy.33
  347.2 8.2 scatter_custom_fusion.4
  355.5 3.4 collective-permute-start.5
  358.9 2.4 fusion.28
  362.1 2.2 multiply_reduce_fusion
  364.5 10.3 %collective-permute-done.5 = f32[256,512]{1,0:T(8,128)} collective-permute-done((f32[256,512]{1,0:T(8,128)}, f32[256,512]{1,0:T(8,128)}, u32[]{:S(2)}, u32[]{:S(2)}) %collective-permute-start.5) | collective-permute-done | bytes 524320 | tf_op jit(solution)/shard_map/ppermute | solution.py:18
  374.8 9.3 scatter_custom_fusion.5
  384.2 3.4 fusion.19
  387.6 1.4 copy.34
  389.0 4.8 add_add_fusion
  393.8 39.3 %all-reduce.9.cloned.1.call-done = f32[256,512]{1,0:T(8,128)} async-done(((f32[256,512]{1,0:T(8,128)}), f32[256,512]{1,0:T(8,128)}) %all-reduce.9.cloned.1.call-update) | async-done | bytes 524304 | tf_op jit(solution)/shard_map/psum | solution.py:106
  434.8 2.0 divide_subtract_fusion
  436.8 559.7 %all-reduce.11.cloned.1.call-done = f32[2,512,512]{2,1,0:T(8,128)} async-done(((f32[2,512,512]{2,1,0:T(8,128)}), f32[2,512,512]{2,1,0:T(8,128)}) %all-reduce.11.cloned.1.call-update) | async-done | bytes 2097168 | tf_op jit(solution)/shard_map/psum | solution.py:109
  996.5 5.0 multiply_subtract_fusion
  (161 shorter events, 34.1 us)
Async XLA Ops:
  8.7 23.9 %all-to-all-start = ((s32[64,1,4]{2,1,0:T(1,128)}), s32[64,1,4]{2,1,0:T(1,128)S(1)}, u32[]{:S(2)}, u32[]{:S(2)}) async-start(s32[64,1,4]{2,1,0:T(1,128)} %bitcast.6), calls=%async_computation | async-start | bytes 65536 | tf_op jit(solution)/shard_map/all_to_all | solution.py:86
  20.1 29.1 %collective-permute-start = (bf16[256,512]{1,0:T(8,128)(2,1)S(1)}, bf16[256,512]{1,0:T(8,128)(2,1)S(1)}, u32[]{:S(2)}, u32[]{:S(2)}) collective-permute-start(bf16[256,512]{1,0:T(8,128)(2,1)S(1)} %convert_element_type.93), channel_id=1, source_target_pairs={{4,0},{8,4},{12,8},{16,12},{20,16},{24,20},{28,24},{32,28},{36,32}... | collective-permute-start | bytes 786440 | tf_op jit(solution)/shard_map/ppermute | solution.py:18
  24.8 2.7 copy-start
  29.1 3.5 copy-start.3
  34.9 20.5 %all-to-all-start.1 = ((bf16[64,4,512]{2,1,0:T(4,128)(2,1)}), bf16[64,4,512]{2,1,0:T(4,128)(2,1)}, u32[]{:S(2)}, u32[]{:S(2)}) async-start(bf16[64,4,512]{2,1,0:T(4,128)(2,1)} %broadcast_select_fusion.8), calls=%async_computation.1 | async-start | bytes 524288 | tf_op jit(solution)/shard_map/all_to_all | solution.py:82
  56.4 2.9 copy-start.20
  56.4 2.9 copy-start.27
  59.3 1.1 copy-start.26
  60.4 1.3 copy-start.10
  61.8 19.7 %copy-start.16 = (bf16[768,512]{1,0:T(8,128)(2,1)S(1)}, bf16[768,512]{1,0:T(8,128)(2,1)}, u32[]{:S(2)}) copy-start(bf16[768,512]{1,0:T(8,128)(2,1)} %broadcast_select_fusion.4) | copy-start | bytes 2359300
  62.7 22.0 %all-to-all-start.2 = ((f32[64,4,512]{2,1,0:T(4,128)}), f32[64,4,512]{2,1,0:T(4,128)S(1)}, u32[]{:S(2)}, u32[]{:S(2)}) async-start(f32[64,4,512]{2,1,0:T(4,128)} %reshape.588), calls=%async_computation.2 | async-start | bytes 1048576 | tf_op jit(solution)/shard_map/all_to_all | solution.py:100
  79.8 17.0 %collective-permute-start.1 = (f32[256,512]{1,0:T(8,128)}, f32[256,512]{1,0:T(8,128)}, u32[]{:S(2)}, u32[]{:S(2)}) collective-permute-start(f32[256,512]{1,0:T(8,128)} %scatter_custom_fusion), channel_id=1, source_target_pairs={{252,0},{0,4},{4,8},{8,12},{12,16},{16,20},{20,24},{24,28},{28,32}... | collective-permute-start | bytes 1572872 | tf_op jit(solution)/shard_map/ppermute | solution.py:18
  84.8 21.5 %all-to-all-start.3 = ((s32[64,1,4]{2,1,0:T(1,128)}), s32[64,1,4]{2,1,0:T(1,128)S(1)}, u32[]{:S(2)}, u32[]{:S(2)}) async-start(s32[64,1,4]{2,1,0:T(1,128)} %bitcast.20), calls=%async_computation.3 | async-start | bytes 65536 | tf_op jit(solution)/shard_map/all_to_all | solution.py:86
  92.9 68.5 %all-reduce.5.cloned.1.call-start = ((), (), s32[]{:S(2)}) async-start(), calls=%async_computation.9 | async-start | bytes 1048576 | tf_op jit(solution)/shard_map/psum | solution.py:106
  96.9 65.7 %copy-start.21 = (f32[256]{0:T(256)S(1)}, f32[256]{0:T(256)}, u32[]{:S(2)}) copy-start(f32[256]{0:T(256)} %param.13) | copy-start | bytes 3076
  96.9 65.7 %copy-start.1 = (f32[256,512]{1,0:T(8,128)S(1)}, f32[256,512]{1,0:T(8,128)}, u32[]{:S(2)}) copy-start(f32[256,512]{1,0:T(8,128)} %param.12) | copy-start | bytes 1572868
  163.7 23.8 %collective-permute-start.2 = (bf16[256,512]{1,0:T(8,128)(2,1)S(1)}, bf16[256,512]{1,0:T(8,128)(2,1)S(1)}, u32[]{:S(2)}, u32[]{:S(2)}) collective-permute-start(bf16[256,512]{1,0:T(8,128)(2,1)S(1)} %fusion.70), channel_id=1, source_target_pairs={{8,0},{12,4},{16,8},{20,12},{24,16},{28,20},{32,24},{36,28},{40,32... | collective-permute-start | bytes 786440 | tf_op jit(solution)/shard_map/ppermute | solution.py:18
  173.5 19.5 %all-to-all-start.4 = ((bf16[64,4,512]{2,1,0:T(4,128)(2,1)}), bf16[64,4,512]{2,1,0:T(4,128)(2,1)S(1)}, u32[]{:S(2)}, u32[]{:S(2)}) async-start(bf16[64,4,512]{2,1,0:T(4,128)(2,1)} %broadcast_select_fusion.7), calls=%async_computation.4 | async-start | bytes 524288 | tf_op jit(solution)/shard_map/all_to_all | solution.py:82
  184.0 3.5 copy-start.5
  193.1 2.9 copy-start.18
  193.1 2.9 copy-start.29
  196.0 1.1 copy-start.25
  197.1 1.3 copy-start.9
  198.5 20.5 %copy-start.19 = (bf16[256,512]{1,0:T(8,128)(2,1)S(1)}, bf16[256,512]{1,0:T(8,128)(2,1)}, u32[]{:S(2)}) copy-start(bf16[256,512]{1,0:T(8,128)(2,1)} %copy-done.18) | copy-start | bytes 786436
  199.4 23.0 %all-to-all-start.5 = ((f32[64,4,512]{2,1,0:T(4,128)}), f32[64,4,512]{2,1,0:T(4,128)S(1)}, u32[]{:S(2)}, u32[]{:S(2)}) async-start(f32[64,4,512]{2,1,0:T(4,128)} %reshape.591), calls=%async_computation.5 | async-start | bytes 1048576 | tf_op jit(solution)/shard_map/all_to_all | solution.py:100
  217.5 18.4 %collective-permute-start.3 = (f32[256,512]{1,0:T(8,128)}, f32[256,512]{1,0:T(8,128)}, u32[]{:S(2)}, u32[]{:S(2)}) collective-permute-start(f32[256,512]{1,0:T(8,128)} %scatter_custom_fusion.2), channel_id=1, source_target_pairs={{248,0},{252,4},{0,8},{4,12},{8,16},{12,20},{16,24},{20,28},{24,32... | collective-permute-start | bytes 1572872 | tf_op jit(solution)/shard_map/ppermute | solution.py:18
  222.5 22.8 %all-to-all-start.6 = ((s32[64,1,4]{2,1,0:T(1,128)}), s32[64,1,4]{2,1,0:T(1,128)S(1)}, u32[]{:S(2)}, u32[]{:S(2)}) async-start(s32[64,1,4]{2,1,0:T(1,128)} %bitcast.29), calls=%async_computation.6 | async-start | bytes 65536 | tf_op jit(solution)/shard_map/all_to_all | solution.py:86
  231.1 65.8 %all-reduce.7.cloned.1.call-start = ((), (), s32[]{:S(2)}) async-start(), calls=%async_computation.10 | async-start | bytes 1048576 | tf_op jit(solution)/shard_map/psum | solution.py:106
  235.9 62.2 %copy-start.2 = (f32[256,512]{1,0:T(8,128)S(1)}, f32[256,512]{1,0:T(8,128)}, u32[]{:S(2)}) copy-start(f32[256,512]{1,0:T(8,128)} %all-reduce.5.cloned.1.call-done) | copy-start | bytes 1572868
  300.2 20.7 %collective-permute-start.4 = (bf16[256,512]{1,0:T(8,128)(2,1)S(1)}, bf16[256,512]{1,0:T(8,128)(2,1)S(1)}, u32[]{:S(2)}, u32[]{:S(2)}) collective-permute-start(bf16[256,512]{1,0:T(8,128)(2,1)S(1)} %get-tuple-element.25), channel_id=1, source_target_pairs={{12,0},{16,4},{20,8},{24,12},{28,16},{32,20},{36,24},{40,28},{44,3... | collective-permute-start | bytes 786440 | tf_op jit(solution)/shard_map/ppermute | solution.py:18
  309.2 15.4 %all-to-all-start.7 = ((bf16[64,4,512]{2,1,0:T(4,128)(2,1)}), bf16[64,4,512]{2,1,0:T(4,128)(2,1)}, u32[]{:S(2)}, u32[]{:S(2)}) async-start(bf16[64,4,512]{2,1,0:T(4,128)(2,1)} %broadcast_select_fusion.6), calls=%async_computation.7 | async-start | bytes 524288 | tf_op jit(solution)/shard_map/all_to_all | solution.py:82
  317.4 3.5 copy-start.7
  325.7 2.9 copy-start.17
  325.7 2.9 copy-start.28
  328.6 1.2 copy-start.24
  329.7 1.3 copy-start.8
  331.0 9.3 copy-start.4
  331.1 11.3 %copy-start.22 = (bf16[768,2]{0,1:T(2,128)(2,1)S(1)}, bf16[768,2]{0,1:T(2,128)(2,1)}, u32[]{:S(2)}) copy-start(bf16[768,2]{0,1:T(2,128)(2,1)} %get-tuple-element.37) | copy-start | bytes 9220
  332.0 32.3 %all-to-all-start.8 = ((f32[64,4,512]{2,1,0:T(4,128)}), f32[64,4,512]{2,1,0:T(4,128)S(1)}, u32[]{:S(2)}, u32[]{:S(2)}) async-start(f32[64,4,512]{2,1,0:T(4,128)} %reshape.594), calls=%async_computation.8 | async-start | bytes 1048576 | tf_op jit(solution)/shard_map/all_to_all | solution.py:100
  340.2 92.9 %all-reduce.9.cloned.1.call-start = ((), (), s32[]{:S(2)}) async-start(), calls=%async_computation.11 | async-start | bytes 1048576 | tf_op jit(solution)/shard_map/psum | solution.py:106
  342.3 3.8 copy-start.6
  347.2 11.6 %copy-start.15 = (bf16[768,512]{1,0:T(8,128)(2,1)S(1)}, bf16[768,512]{1,0:T(8,128)(2,1)}, u32[]{:S(2)}) copy-start(bf16[768,512]{1,0:T(8,128)(2,1)} %broadcast_select_fusion) | copy-start | bytes 2359300
  355.5 6.7 copy-start.12
  355.5 19.3 %collective-permute-start.5 = (f32[256,512]{1,0:T(8,128)}, f32[256,512]{1,0:T(8,128)}, u32[]{:S(2)}, u32[]{:S(2)}) collective-permute-start(f32[256,512]{1,0:T(8,128)} %scatter_custom_fusion.4), channel_id=1, source_target_pairs={{244,0},{248,4},{252,8},{0,12},{4,16},{8,20},{12,24},{16,28},{20,3... | collective-permute-start | bytes 1572872 | tf_op jit(solution)/shard_map/ppermute | solution.py:18
  361.3 0.9 copy-start.13
  364.3 19.9 %copy-start.23 = (bf16[768,2]{0,1:T(2,128)(2,1)S(1)}, bf16[768,2]{0,1:T(2,128)(2,1)}, u32[]{:S(2)}) copy-start(bf16[768,2]{0,1:T(2,128)(2,1)} %get-tuple-element.35) | copy-start | bytes 9220
  364.5 19.7 %copy-start.14 = (bf16[768,512]{0,1:T(8,128)(2,1)S(1)}, bf16[768,512]{0,1:T(8,128)(2,1)}, u32[]{:S(2)}) copy-start(bf16[768,512]{0,1:T(8,128)(2,1)} %copy.33) | copy-start | bytes 2359300
  384.1 612.4 %all-reduce.11.cloned.1.call-start = ((), (), s32[]{:S(2)}) async-start(), calls=%async_computation.12 | async-start | bytes 4194304 | tf_op jit(solution)/shard_map/psum | solution.py:109
  393.8 41.0 %copy-start.11 = (f32[256,512]{1,0:T(8,128)S(1)}, f32[256,512]{1,0:T(8,128)}, u32[]{:S(2)}) copy-start(f32[256,512]{1,0:T(8,128)} %get-tuple-element.26) | copy-start | bytes 1572868
Sparse Core Ops, SparseCore 0:
  106.4 54.9 all-reduce.4
  245.4 51.5 all-reduce.6
  384.2 48.7 all-reduce.8
  436.1 560.3 all-reduce.10
where the time goes:
time: 1020 us; the launch traced here: 1010 us
  waiting for transfers between devices  718 us (70%)
  starting transfers between devices  93.1 us (9%)
  other arithmetic  82 us (8%)
  matrix products  52.8 us (5%)
  local copies, waits for them, and re-layouts  47.4 us (5%)
  between operations  15 us (1%)
    psum x1, waiting for transfers between devices, on_device(): summed = lax.psum(rel_total, 'dom')  560 us
    psum x3, waiting for transfers between devices, on_device(): summed = lax.psum(grads, 'rep')  146 us
    scatter-add x3, other arithmetic, on_device(): returned.at[jnp.concatenate([head_idx, served.reshape(-1)])]  28 us
    all_to_all x3, starting transfers between devices, on_device(): lax.all_to_all(requests, 'dom', split_axis=0, concat_axis=0, tiled=True)  27.1 us
    scatter-add x3, other arithmetic, on_device(): tail_block = jnp.zeros((rows, width), jnp.float32).at[tail_idx].add(dtail)  24.6 us
    all_to_all x3, starting transfers between devices, on_device(): lax.all_to_all(dneg.reshape(parts, NCAP, width), 'dom', split_axis=0, con...  24.1 us
    all_to_all x3, starting transfers between devices, fetch(): lax.all_to_all(taken, 'dom', split_axis=0, concat_axis=0, tiled=True)  21.8 us
  transfers between devices with their start and end apart: 19, of which 6 were waited for; matrix products, arithmetic and copies ran while one was open for 14% of the time, Pallas kernels for 0%

commit v1 on v0

v1 whole, which is shorter than its diff:
```python
import jax
import jax.numpy as jnp
from jax import lax
from jax.experimental import pallas as pl
from jax.experimental.pallas import tpu as pltpu
from jax.sharding import PartitionSpec as P

NCAP = 4
ROUNDS = 3
LANES = 128

negative_weight = 0.0625
entity_rate = 0.05
relation_rate = 0.02

BF = jnp.bfloat16
F32 = jnp.float32


def call(kernel, outs, *args, flops=0, aliases=None, vmem=24):
    outs = [jax.ShapeDtypeStruct(s, d) for s, d in outs]
    moved = sum(a.size * a.dtype.itemsize for a in args)
    moved += sum(o.size * o.dtype.itemsize for o in outs)
    return pl.pallas_call(
        kernel,
        out_shape=outs,
        in_specs=[pl.BlockSpec(memory_space=pltpu.VMEM)] * len(args),
        out_specs=[pl.BlockSpec(memory_space=pltpu.VMEM)] * len(outs),
        input_output_aliases=aliases or {},
        compiler_params=pltpu.CompilerParams(vmem_limit_bytes=vmem << 20),
        cost_estimate=pl.CostEstimate(flops=flops, bytes_accessed=moved, transcendentals=0),
    )(*args)


def nn(a, b):
    return jnp.dot(a, b, preferred_element_type=F32)


def nt(a, b):
    return lax.dot_general(a, b, (((1,), (1,)), ((), ())), preferred_element_type=F32)


def tn(a, b):
    return lax.dot_general(a, b, (((0,), (0,)), ((), ())), preferred_element_type=F32)


def iota(shape, dim):
    return lax.broadcasted_iota(jnp.int32, shape, dim)


def one_hot_rows(count, index):
    return (iota((count, index.shape[1]), 0) == index).astype(F32).astype(BF)


def all_ways(block, axes):
    return lax.all_to_all(block, axes, split_axis=0, concat_axis=0, tiled=True)


def from_behind(block, axis, distance):
    n = lax.axis_size(axis)
    return lax.ppermute(block, axis, [((i - distance) % n, i) for i in range(n)])


def fill_container(out_ref, ent_bf, idx_x):
    width = ent_bf.shape[1]
    cuts = width // LANES
    picked = tn(one_hot_rows(ent_bf.shape[0], idx_x), ent_bf)
    which = (iota((idx_x.shape[1], LANES), 0) // NCAP) % cuts
    out = picked[:, :LANES]
    for cs in range(1, cuts):
        out = jnp.where(which == cs, picked[:, cs * LANES : (cs + 1) * LANES], out)
    out_ref[...] = out.astype(BF)


def serve_kernel(ent_ref, idx_ref, out_ref):
    fill_container(out_ref, ent_ref[...], idx_ref[...])


def tail_kernel(ent_ref, rel_ref, par_ref, head_ref, tail_ref, kind_ref, tq_ref, at_ref, n_ref, dtail_ref):
    rows = ent_ref.shape[0]
    kinds = rel_ref.shape[0]
    ent = ent_ref[...]
    for t in range(kinds):
        tq_ref[t * rows : (t + 1) * rows, :] = nn(ent, rel_ref[t]).astype(BF)
    pick_q = one_hot_rows(kinds * rows, kind_ref[...] * rows + head_ref[...])
    pick_t = one_hot_rows(rows, tail_ref[...])
    ones = jnp.ones((LANES, pick_q.shape[1]), F32).astype(BF)
    joint = nt(pick_q, pick_t)
    n = nt(pick_q, ones)
    c = nt(ones, pick_t)[:1]
    n_ref[...] = n
    tq = tq_ref[...]
    par = par_ref[...]
    prob = jax.nn.sigmoid(nt(tq, par))
    weight = (negative_weight * n[:, :1]) * c
    at = (weight * prob + joint * ((1.0 - negative_weight) * prob - 1.0)).astype(BF)
    at_ref[...] = at
    dtail_ref[...] = tn(at, tq).astype(BF)


def neg_kernel(con_ref, tq_ref, n_ref, neg_ref, an_ref, dneg_ref):
    slots, width = neg_ref.shape
    cuts = width // LANES
    con = con_ref[...]
    slot = iota((slots, con.shape[0]), 0)
    row = iota((slots, con.shape[0]), 1) - ((slot // NCAP) * (NCAP * cuts) + slot % NCAP)
    for cs in range(cuts):
        perm = (row == cs * NCAP).astype(F32).astype(BF)
        neg_ref[:, cs * LANES : (cs + 1) * LANES] = nn(perm, con).astype(BF)
    tq = tq_ref[...]
    prob = jax.nn.sigmoid(nt(tq, neg_ref[...]))
    an = (negative_weight * n_ref[:, :1] * prob).astype(BF)
    an_ref[...] = an
    dneg = tn(an, tq).astype(BF)
    wide = dneg_ref.shape[1]
    for cs in range(width // wide):
        dneg_ref[cs * slots : (cs + 1) * slots, :] = dneg[:, cs * wide : (cs + 1) * wide]


def head_kernel(at_ref, an_ref, par_ref, neg_ref, rel_ref, tail_ref, g_ref, out_ref):
    rows = par_ref.shape[0]
    kinds = rel_ref.shape[0]
    g = (nn(at_ref[...], par_ref[...]) + nn(an_ref[...], neg_ref[...])).astype(BF)
    g_ref[...] = g
    total = tail_ref[...].astype(F32)
    for t in range(kinds):
        total = total + nt(g[t * rows : (t + 1) * rows], rel_ref[t])
    wide = out_ref.shape[2]
    for cs in range(out_ref.shape[0]):
        out_ref[cs] = total[:, cs * wide : (cs + 1) * wide].astype(BF)


def rel_kernel(first, *refs):
    ent_ref, g_ref = refs[:2]
    out_ref = refs[-1]
    rows = ent_ref.shape[0]
    ent = ent_ref[...]
    for t in range(out_ref.shape[0]):
        part = tn(ent, g_ref[t * rows : (t + 1) * rows])
        if not first:
            part = part + refs[2][t]
        out_ref[t] = part.astype(out_ref.dtype)


def join_kernel(parts_ref, neg_ref, idx_ref, out_ref):
    rows = parts_ref.shape[1]
    total = nn(one_hot_rows(rows, idx_ref[...]), neg_ref[...])
    for j in range(parts_ref.shape[0]):
        total = total + parts_ref[j].astype(F32)
    total = total.astype(BF)
    for j in range(out_ref.shape[0]):
        out_ref[j] = total


def update(grad_ref, ent_ref, acc_ref, new_ref, new_acc_ref):
    cuts, _, wide = grad_ref.shape
    grads = [grad_ref[j].astype(F32) for j in range(cuts)]
    square = sum(jnp.sum(g * g, axis=-1, keepdims=True) for g in grads)
    acc = acc_ref[...] + square / (cuts * wide)
    new_acc_ref[...] = acc
    scale = entity_rate / jnp.sqrt(acc)
    for j in range(cuts):
        cut = slice(j * wide, (j + 1) * wide)
        new_ref[:, cut] = ent_ref[:, cut] - scale * grads[j]


def update_kernel(grad_ref, ent_ref, acc_ref, idx_ref, new_ref, new_acc_ref, bf_ref, con_ref):
    update(grad_ref, ent_ref, acc_ref, new_ref, new_acc_ref)
    bf = new_ref[...].astype(BF)
    bf_ref[...] = bf
    fill_container(con_ref, bf, idx_ref[...])


def total_kernel(parts_ref, out_ref):
    total = jnp.sum(parts_ref[...].astype(F32), axis=0).astype(BF)
    out_ref[...] = jnp.broadcast_to(total[None], out_ref.shape)


def on_device(entities, ent_accum, relations, rel_accum, heads, tails, relation_ids, negatives):
    rows, width = entities.shape
    parts = lax.axis_size("dom")
    reps = lax.axis_size("rep")
    kinds = relations.shape[0]
    slots = parts * NCAP
    wide = width // reps
    cuts = width // LANES
    everyone = ("rep", "dom")
    mine = lax.axis_index("rep")

    asked = negatives.reshape(ROUNDS, parts, NCAP).transpose(1, 0, 2).reshape(1, parts, ROUNDS * NCAP)
    asked = jnp.broadcast_to(asked, (reps, parts, ROUNDS * NCAP)).reshape(reps * parts, ROUNDS * NCAP)
    asked = all_ways(asked, everyone).reshape(reps, parts, ROUNDS, NCAP)
    served_all = asked.transpose(2, 0, 1, 3).reshape(ROUNDS, 1, reps * slots)
    own = lax.dynamic_index_in_dim(asked, mine, 0, keepdims=False).transpose(1, 0, 2)
    own = jnp.broadcast_to(own[:, :, None, :], (ROUNDS, parts, cuts, NCAP)).reshape(
        ROUNDS, 1, parts * cuts * NCAP
    )

    rel_bf = relations.astype(BF)
    ent_bf = entities.astype(BF)
    accum = ent_accum.reshape(rows, 1)
    con = None
    drel = None
    for rnd in range(ROUNDS):
        offset = rnd + 1
        last = rnd == ROUNDS - 1
        if rnd == 0:
            (con,) = call(serve_kernel, [((parts * cuts * NCAP, LANES), BF)], ent_bf, own[0])
        partner = from_behind(ent_bf, "dom", -offset)
        con = all_ways(con.reshape(parts, cuts * NCAP, LANES), "dom").reshape(parts * cuts * NCAP, LANES)
        tq, at, n, dtail = call(
            tail_kernel,
            [((kinds * rows, width), BF), ((kinds * rows, rows), BF), ((kinds * rows, LANES), F32), ((rows, width), BF)],
            ent_bf,
            rel_bf,
            partner,
            heads[rnd : rnd + 1],
            tails[rnd : rnd + 1],
            relation_ids[rnd : rnd + 1],
        )
        dtail = from_behind(dtail, "dom", offset)
        neg, an, dneg = call(
            neg_kernel,
            [((slots, width), BF), ((kinds * rows, slots), BF), ((reps * slots, wide), BF)],
            con,
            tq,
            n,
        )
        dneg = all_ways(dneg.reshape(reps * parts, NCAP, wide), everyone).reshape(reps * slots, wide)
        g, dhead = call(
            head_kernel,
            [((kinds * rows, width), BF), ((reps, rows, wide), BF)],
            at,
            an,
            partner,
            neg,
            rel_bf,
            dtail,
        )
        dhead = all_ways(dhead, "rep")
        args = (ent_bf, g) if rnd == 0 else (ent_bf, g, drel)
        (drel,) = call(
            lambda *refs, first=rnd == 0: rel_kernel(first, *refs),
            [((kinds, width, width), BF if last else F32)],
            *args,
            aliases={2: 0} if rnd > 0 and not last else None,
        )
        (grads,) = call(join_kernel, [((reps, rows, wide), BF)], dhead, dneg, served_all[rnd])
        grads = all_ways(grads, "rep")
        if last:
            entities, accum = call(update, [((rows, width), F32), ((rows, 1), F32)], grads, entities, accum)
        else:
            entities, accum, ent_bf, con = call(
                update_kernel,
                [((rows, width), F32), ((rows, 1), F32), ((rows, width), BF), ((parts * cuts * NCAP, LANES), BF)],
                grads,
                entities,
                accum,
                own[rnd + 1],
            )
    piece = kinds * width // parts
    drel = all_ways(drel.reshape(parts, piece, width), "dom")
    (total,) = call(total_kernel, [((parts, piece, width), BF)], drel)
    total = all_ways(total, "dom").reshape(kinds, width, width).astype(F32)
    new_rel_accum = rel_accum + total * total
    new_relations = relations - relation_rate * total / jnp.sqrt(new_rel_accum)
    return (entities, accum.reshape(rows), new_relations, new_rel_accum)


def solution(mesh):
    in_specs = (
        P("dom", None),
        P("dom"),
        P("rep", None, None),
        P("rep", None, None),
        P(None, ("dom", "rep")),
        P(None, ("dom", "rep")),
        P(None, ("dom", "rep")),
        P(None, ("dom", "rep")),
    )
    out_specs = (P("dom", None), P("dom"), P("rep", None, None), P("rep", None, None))
    return jax.shard_map(
        on_device, mesh=mesh, in_specs=in_specs, out_specs=out_specs, check_vma=False
    )
```

time: 1020 us -> 309 us (0.30)
  waiting for transfers between devices: 718 us -> 132 us
  other arithmetic: 82 us -> 7.05 us
  matrix products: 52.8 us -> 0 us
  blocking collectives: 0 us -> 37.1 us
  local copies, waits for them, and re-layouts: 47.4 us -> 14.4 us
  Pallas kernels: 0 us -> 25.9 us
  between operations: 15 us -> 1.07 us
    psum x4 -> x0, waiting for transfers between devices: 705 us -> none  [the longest x1 560 us: on_device(): summed = lax.psum(rel_total, 'dom')]
    all_to_all x9 -> x12, waiting for transfers between devices: 2.36 us -> 121 us  [all_ways(): return lax.all_to_all(block, axes, split_axis=0, concat_axis=0, tiled=True)]
    dot_general x18 -> x0, matrix products: 52.8 us -> none  [the longest x3 11.9 us: bucket_terms(): lax.dot_general(masked, dquery, (((0,), (0,)), ((), ())), preferred_eleme...]
    scatter-add x6 -> x0, other arithmetic: 52.6 us -> none  [the longest x3 28 us: on_device(): returned.at[jnp.concatenate([head_idx, served.reshape(-1)])]]
    all_to_all x0 -> x3, blocking collectives: none -> 37.1 us  [all_ways(): return lax.all_to_all(block, axes, split_axis=0, concat_axis=0, tiled=True)]
    pallas_call x0 -> x20, Pallas kernels: none -> 25.9 us  [call(): pl.pallas_call(kernel, out_shape=outs, in_specs=[pl.BlockSpec(memory_spac...]
    gather x12 -> x0, local copies, waits for them, and re-layouts: 21.7 us -> none  [the longest x3 8.69 us: on_device(): jnp.take(ent_bf, head_idx, axis=0)]
    select_n x22 -> x0, other arithmetic: 10.6 us -> none  [the longest x6 4.36 us: on_device(): jnp.take(partner, tail_idx, axis=0)]
  transfers between devices with their start and end apart: 19 -> 18, of which waited for: 6 -> 15; matrix products, arithmetic and copies ran while one was open for 14% -> 2% of each run, Pallas kernels for 0% -> 6%
where the time goes in v1:
time: 309 us; the launch traced here: 308 us
  waiting for transfers between devices  132 us (43%)
  starting transfers between devices  89.7 us (29%)
  blocking collectives  37.1 us (12%)
  Pallas kernels  25.9 us (8%)
  local copies, waits for them, and re-layouts  14.4 us (5%)
  other arithmetic  7.05 us (2%)
    all_to_all x12, waiting for transfers between devices, all_ways(): return lax.all_to_all(block, axes, split_axis=0, concat_axis=0, tiled=True)  121 us
    all_to_all x12, starting transfers between devices, all_ways(): return lax.all_to_all(block, axes, split_axis=0, concat_axis=0, tiled=True)  73.8 us
    all_to_all x3, blocking collectives, all_ways(): return lax.all_to_all(block, axes, split_axis=0, concat_axis=0, tiled=True)  37.1 us
    pallas_call x20, Pallas kernels, call(): pl.pallas_call(kernel, out_shape=outs, in_specs=[pl.BlockSpec(memory_spac...  25.9 us
    ppermute x6, starting transfers between devices, from_behind(): lax.ppermute(block, axis, [((i - distance) % n, i) for i in range(n)])  15.9 us
    ppermute x6, waiting for transfers between devices, from_behind(): lax.ppermute(block, axis, [((i - distance) % n, i) for i in range(n)])  11.4 us
    unnamed x47, local copies, waits for them, and re-layouts  9.64 us
  transfers between devices with their start and end apart: 18, of which 15 were waited for; matrix products, arithmetic and copies ran while one was open for 2% of the time, Pallas kernels for 6%

profile of v1, /device:TPU:1, one launch (start us, length us, event | category | flops | bytes accessed | tf_op | source)
XLA Modules:
  0.0 307.5 jit_solution(11344796932474814326)
XLA Ops:
  0.6 0.8 reshape.98
  2.3 15.6 %all-to-all-start = ((s32[256,1,12]{2,1,0:T(1,128)}), s32[256,1,12]{2,1,0:T(1,128)S(1)}, u32[]{:S(2)}, u32[]{:S(2)}) async-start(s32[256,1,12]{2,1,0:T(1,128)} %bitcast.1), calls=%async_computation | async-start | bytes 262144 | tf_op jit(solution)/shard_map/all_to_all | solution.py:56
  18.0 1.1 convert_element_type.10.ent_ref.refs_0_
  19.1 2.2 collective-permute-start
  21.3 9.5 %all-to-all-done = s32[256,1,12]{2,1,0:T(1,128)S(1)} async-done(((s32[256,1,12]{2,1,0:T(1,128)}), s32[256,1,12]{2,1,0:T(1,128)S(1)}, u32[]{:S(2)}, u32[]{:S(2)}) %all-to-all-start) | async-done | bytes 12320 | tf_op jit(solution)/shard_map/all_to_all | solution.py:56
  31.2 1.2 shard_map.112
  32.4 5.4 %all-to-all-start.1 = ((bf16[64,16,128]{2,1,0:T(8,128)(2,1)}), bf16[64,16,128]{2,1,0:T(8,128)(2,1)S(1)}, u32[]{:S(2)}, u32[]{:S(2)}) async-start(bf16[64,16,128]{2,1,0:T(8,128)(2,1)} %bitcast.5), calls=%async_computation.1 | async-start | bytes 524288 | tf_op jit(solution)/shard_map/all_to_all | solution.py:56
  37.8 1.7 convert_element_type.11.rel_ref
  39.6 1.5 shard_map.111
  41.1 1.7 collective-permute-start.1
  42.8 4.8 %all-to-all-done.1 = bf16[64,16,128]{2,1,0:T(8,128)(2,1)S(1)} async-done(((bf16[64,16,128]{2,1,0:T(8,128)(2,1)}), bf16[64,16,128]{2,1,0:T(8,128)(2,1)S(1)}, u32[]{:S(2)}, u32[]{:S(2)}) %all-to-all-start.1) | async-done | bytes 262176 | tf_op jit(solution)/shard_map/all_to_all | solution.py:56
  47.6 2.1 shard_map.113
  51.2 11.5 %all_to_all.79.parts_ref = bf16[4,256,128]{2,1,0:T(8,128)(2,1)S(1)} all-to-all(bf16[4,256,128]{2,1,0:T(8,128)(2,1)S(1)} %get-tuple-element.47), channel_id=1, replica_groups=mesh['dom'=64,'rep'=4] {'rep'}, dimensions={0} | all-to-all | bytes 524288 | tf_op jit(solution)/shard_map/all_to_all | solution.py:56
  62.7 8.2 %all-to-all-start.3 = ((bf16[256,4,128]{2,1,0:T(4,128)(2,1)}), bf16[256,4,128]{2,1,0:T(4,128)(2,1)S(1)}, u32[]{:S(2)}, u32[]{:S(2)}) async-start(bf16[256,4,128]{2,1,0:T(4,128)(2,1)} %bitcast.7), calls=%async_computation.3 | async-start | bytes 524288 | tf_op jit(solution)/shard_map/all_to_all | solution.py:56
  71.7 14.7 %all-to-all-done.3 = bf16[256,4,128]{2,1,0:T(4,128)(2,1)S(1)} async-done(((bf16[256,4,128]{2,1,0:T(4,128)(2,1)}), bf16[256,4,128]{2,1,0:T(4,128)(2,1)S(1)}, u32[]{:S(2)}, u32[]{:S(2)}) %all-to-all-start.3) | async-done | bytes 262176 | tf_op jit(solution)/shard_map/all_to_all | solution.py:56
  86.5 1.0 shard_map.115
  87.5 3.4 %all-to-all-start.4 = ((bf16[4,256,128]{2,1,0:T(8,128)(2,1)}), bf16[4,256,128]{2,1,0:T(8,128)(2,1)S(1)}, u32[]{:S(2)}, u32[]{:S(2)}) async-start(bf16[4,256,128]{2,1,0:T(8,128)(2,1)} %shard_map.115), calls=%async_computation.4 | async-start | bytes 524288 | tf_op jit(solution)/shard_map/all_to_all | solution.py:56
  91.3 8.0 %all-to-all-done.4.grad_ref = bf16[4,256,128]{2,1,0:T(8,128)(2,1)S(1)} async-done(((bf16[4,256,128]{2,1,0:T(8,128)(2,1)}), bf16[4,256,128]{2,1,0:T(8,128)(2,1)S(1)}, u32[]{:S(2)}, u32[]{:S(2)}) %all-to-all-start.4) | async-done | bytes 262176 | tf_op jit(solution)/shard_map/all_to_all | solution.py:56
  99.4 1.5 shard_map.116
  100.8 3.9 %collective-permute-start.2 = (bf16[256,512]{1,0:T(8,128)(2,1)S(1)}, bf16[256,512]{1,0:T(8,128)(2,1)S(1)}, u32[]{:S(2)}, u32[]{:S(2)}) collective-permute-start(bf16[256,512]{1,0:T(8,128)(2,1)S(1)} %get-tuple-element.49.ent_ref.refs_0_), channel_id=1, source_target_pairs={{8,0},{12,4},{16,8},{20,12},{24,16},{28,20},{32,24},{36,28},{40,32... | collective-permute-start | bytes 786440 | tf_op jit(solution)/shard_map/ppermute | solution.py:61
  104.7 5.8 %all-to-all-start.5 = ((bf16[64,16,128]{2,1,0:T(8,128)(2,1)}), bf16[64,16,128]{2,1,0:T(8,128)(2,1)S(1)}, u32[]{:S(2)}, u32[]{:S(2)}) async-start(bf16[64,16,128]{2,1,0:T(8,128)(2,1)} %bitcast.13), calls=%async_computation.5 | async-start | bytes 524288 | tf_op jit(solution)/shard_map/all_to_all | solution.py:56
  110.5 2.2 shard_map.117
  113.4 1.4 collective-permute-start.3
  114.7 5.6 %all-to-all-done.5 = bf16[64,16,128]{2,1,0:T(8,128)(2,1)S(1)} async-done(((bf16[64,16,128]{2,1,0:T(8,128)(2,1)}), bf16[64,16,128]{2,1,0:T(8,128)(2,1)S(1)}, u32[]{:S(2)}, u32[]{:S(2)}) %all-to-all-start.5) | async-done | bytes 262176 | tf_op jit(solution)/shard_map/all_to_all | solution.py:56
  120.4 0.9 copy-done.11
  121.3 1.4 shard_map.118
  122.7 2.5 collective-permute-done.3.tail_ref
  125.2 1.7 shard_map.119
  126.9 12.4 %all_to_all.80.parts_ref = bf16[4,256,128]{2,1,0:T(8,128)(2,1)S(1)} all-to-all(bf16[4,256,128]{2,1,0:T(8,128)(2,1)S(1)} %get-tuple-element.57), channel_id=1, replica_groups=mesh['dom'=64,'rep'=4] {'rep'}, dimensions={0} | all-to-all | bytes 524288 | tf_op jit(solution)/shard_map/all_to_all | solution.py:56
  139.2 7.6 %all-to-all-start.7 = ((bf16[256,4,128]{2,1,0:T(4,128)(2,1)}), bf16[256,4,128]{2,1,0:T(4,128)(2,1)S(1)}, u32[]{:S(2)}, u32[]{:S(2)}) async-start(bf16[256,4,128]{2,1,0:T(4,128)(2,1)} %bitcast.52), calls=%async_computation.7 | async-start | bytes 524288 | tf_op jit(solution)/shard_map/all_to_all | solution.py:56
  146.8 0.8 copy.33
  147.7 14.6 %all-to-all-done.7 = bf16[256,4,128]{2,1,0:T(4,128)(2,1)S(1)} async-done(((bf16[256,4,128]{2,1,0:T(4,128)(2,1)}), bf16[256,4,128]{2,1,0:T(4,128)(2,1)S(1)}, u32[]{:S(2)}, u32[]{:S(2)}) %all-to-all-start.7) | async-done | bytes 262176 | tf_op jit(solution)/shard_map/all_to_all | solution.py:56
  162.4 1.0 shard_map.120
  163.4 3.4 %all-to-all-start.8 = ((bf16[4,256,128]{2,1,0:T(8,128)(2,1)}), bf16[4,256,128]{2,1,0:T(8,128)(2,1)S(1)}, u32[]{:S(2)}, u32[]{:S(2)}) async-start(bf16[4,256,128]{2,1,0:T(8,128)(2,1)} %shard_map.120), calls=%async_computation.8 | async-start | bytes 524288 | tf_op jit(solution)/shard_map/all_to_all | solution.py:56
  167.1 8.2 %all-to-all-done.8.grad_ref = bf16[4,256,128]{2,1,0:T(8,128)(2,1)S(1)} async-done(((bf16[4,256,128]{2,1,0:T(8,128)(2,1)}), bf16[4,256,128]{2,1,0:T(8,128)(2,1)S(1)}, u32[]{:S(2)}, u32[]{:S(2)}) %all-to-all-start.8) | async-done | bytes 262176 | tf_op jit(solution)/shard_map/all_to_all | solution.py:56
  175.3 0.9 copy-done.15
  177.0 0.8 copy-done.1
  177.8 5.0 %collective-permute-start.4 = (bf16[256,512]{1,0:T(8,128)(2,1)S(1)}, bf16[256,512]{1,0:T(8,128)(2,1)S(1)}, u32[]{:S(2)}, u32[]{:S(2)}) collective-permute-start(bf16[256,512]{1,0:T(8,128)(2,1)S(1)} %get-tuple-element.61.ent_ref.refs_0_), channel_id=1, source_target_pairs={{12,0},{16,4},{20,8},{24,12},{28,16},{32,20},{36,24},{40,28},{44,3... | collective-permute-start | bytes 786440 | tf_op jit(solution)/shard_map/ppermute | solution.py:61
  182.8 4.2 %all-to-all-start.9 = ((bf16[64,16,128]{2,1,0:T(8,128)(2,1)}), bf16[64,16,128]{2,1,0:T(8,128)(2,1)S(1)}, u32[]{:S(2)}, u32[]{:S(2)}) async-start(bf16[64,16,128]{2,1,0:T(8,128)(2,1)} %bitcast.51), calls=%async_computation.9 | async-start | bytes 524288 | tf_op jit(solution)/shard_map/all_to_all | solution.py:56
  186.9 2.0 collective-permute-done.4.par_ref
  189.0 2.2 shard_map.122
  192.6 1.7 collective-permute-start.5
  194.3 1.9 all-to-all-done.9
  196.2 0.9 copy-done.13
  197.1 1.4 shard_map.123
  198.5 6.9 %collective-permute-done.5.tail_ref = bf16[256,512]{1,0:T(8,128)(2,1)} collective-permute-done((bf16[256,512]{1,0:T(8,128)(2,1)}, bf16[256,512]{1,0:T(8,128)(2,1)}, u32[]{:S(2)}, u32[]{:S(2)}) %collective-permute-start.5) | collective-permute-done | bytes 262176 | tf_op jit(solution)/shard_map/ppermute | solution.py:61
  205.4 0.9 copy-done.6
  206.3 1.7 shard_map.124
  208.0 13.3 %all_to_all.81.parts_ref = bf16[4,256,128]{2,1,0:T(8,128)(2,1)S(1)} all-to-all(bf16[4,256,128]{2,1,0:T(8,128)(2,1)S(1)} %get-tuple-element.69), channel_id=1, replica_groups=mesh['dom'=64,'rep'=4] {'rep'}, dimensions={0} | all-to-all | bytes 524288 | tf_op jit(solution)/shard_map/all_to_all | solution.py:56
  221.3 5.7 %all-to-all-start.11 = ((bf16[256,4,128]{2,1,0:T(4,128)(2,1)}), bf16[256,4,128]{2,1,0:T(4,128)(2,1)S(1)}, u32[]{:S(2)}, u32[]{:S(2)}) async-start(bf16[256,4,128]{2,1,0:T(4,128)(2,1)} %bitcast.50), calls=%async_computation.11 | async-start | bytes 524288 | tf_op jit(solution)/shard_map/all_to_all | solution.py:56
  227.0 1.0 copy-done.4
  229.0 1.4 shard_map.129
  230.5 12.1 %all-to-all-done.11 = bf16[256,4,128]{2,1,0:T(4,128)(2,1)S(1)} async-done(((bf16[256,4,128]{2,1,0:T(4,128)(2,1)}), bf16[256,4,128]{2,1,0:T(4,128)(2,1)S(1)}, u32[]{:S(2)}, u32[]{:S(2)}) %all-to-all-start.11) | async-done | bytes 262176 | tf_op jit(solution)/shard_map/all_to_all | solution.py:56
  242.6 5.2 %all-to-all-start.13 = ((bf16[64,16,512]{2,1,0:T(8,128)(2,1)}), bf16[64,16,512]{2,1,0:T(8,128)(2,1)S(1)}, u32[]{:S(2)}, u32[]{:S(2)}) async-start(bf16[64,16,512]{2,1,0:T(8,128)(2,1)} %bitcast.22), calls=%async_computation.13 | async-start | bytes 2097152 | tf_op jit(solution)/shard_map/all_to_all | solution.py:56
  248.1 1.0 shard_map.125
  249.1 16.6 %all-to-all-done.13.parts_ref = bf16[64,16,512]{2,1,0:T(8,128)(2,1)S(1)} async-done(((bf16[64,16,512]{2,1,0:T(8,128)(2,1)}), bf16[64,16,512]{2,1,0:T(8,128)(2,1)S(1)}, u32[]{:S(2)}, u32[]{:S(2)}) %all-to-all-start.13) | async-done | bytes 1048608 | tf_op jit(solution)/shard_map/all_to_all | solution.py:56
  265.7 3.4 %all-to-all-start.12 = ((bf16[4,256,128]{2,1,0:T(8,128)(2,1)}), bf16[4,256,128]{2,1,0:T(8,128)(2,1)S(1)}, u32[]{:S(2)}, u32[]{:S(2)}) async-start(bf16[4,256,128]{2,1,0:T(8,128)(2,1)} %shard_map.125), calls=%async_computation.12 | async-start | bytes 524288 | tf_op jit(solution)/shard_map/all_to_all | solution.py:56
  269.2 1.2 shard_map.130
  270.4 8.6 %all-to-all-done.12.grad_ref = bf16[4,256,128]{2,1,0:T(8,128)(2,1)S(1)} async-done(((bf16[4,256,128]{2,1,0:T(8,128)(2,1)}), bf16[4,256,128]{2,1,0:T(8,128)(2,1)S(1)}, u32[]{:S(2)}, u32[]{:S(2)}) %all-to-all-start.12) | async-done | bytes 262176 | tf_op jit(solution)/shard_map/all_to_all | solution.py:56
  279.0 5.9 %all-to-all-start.14 = ((bf16[64,16,512]{2,1,0:T(8,128)(2,1)}), bf16[64,16,512]{2,1,0:T(8,128)(2,1)S(1)}, u32[]{:S(2)}, u32[]{:S(2)}) async-start(bf16[64,16,512]{2,1,0:T(8,128)(2,1)} %shard_map.130), calls=%async_computation.14 | async-start | bytes 2097152 | tf_op jit(solution)/shard_map/all_to_all | solution.py:56
  285.0 1.1 shard_map.126
  286.8 16.1 %all-to-all-done.14 = bf16[64,16,512]{2,1,0:T(8,128)(2,1)S(1)} async-done(((bf16[64,16,512]{2,1,0:T(8,128)(2,1)}), bf16[64,16,512]{2,1,0:T(8,128)(2,1)S(1)}, u32[]{:S(2)}, u32[]{:S(2)}) %all-to-all-start.14) | async-done | bytes 1048608 | tf_op jit(solution)/shard_map/all_to_all | solution.py:56
  303.5 1.0 copy-done.17
  304.5 3.0 fusion
  (74 shorter events, 9.9 us)
Async XLA Ops:
  0.6 37.2 %copy-start.19 = (s32[3,768]{1,0:T(4,128)S(1)}, s32[3,768]{1,0:T(4,128)}, u32[]{:S(2)}) copy-start(s32[3,768]{1,0:T(4,128)} %param.12) | copy-start | bytes 27652
  2.3 28.4 %all-to-all-start = ((s32[256,1,12]{2,1,0:T(1,128)}), s32[256,1,12]{2,1,0:T(1,128)S(1)}, u32[]{:S(2)}, u32[]{:S(2)}) async-start(s32[256,1,12]{2,1,0:T(1,128)} %bitcast.1), calls=%async_computation | async-start | bytes 262144 | tf_op jit(solution)/shard_map/all_to_all | solution.py:56
  19.1 20.6 %collective-permute-start = (bf16[256,512]{1,0:T(8,128)(2,1)S(1)}, bf16[256,512]{1,0:T(8,128)(2,1)S(1)}, u32[]{:S(2)}, u32[]{:S(2)}) collective-permute-start(bf16[256,512]{1,0:T(8,128)(2,1)S(1)} %convert_element_type.10.ent_ref.refs_0_), channel_id=1, source_target_pairs={{4,0},{8,4},{12,8},{16,12},{20,16},{24,20},{28,24},{32,28},{36,32}... | collective-permute-start | bytes 786440 | tf_op jit(solution)/shard_map/ppermute | solution.py:61
  31.2 8.3 %copy-start.20 = (s32[3,768]{1,0:T(4,128)S(1)}, s32[3,768]{1,0:T(4,128)}, u32[]{:S(2)}) copy-start(s32[3,768]{1,0:T(4,128)} %param.14) | copy-start | bytes 27652
  31.2 8.4 %copy-start.21 = (s32[3,768]{1,0:T(4,128)S(1)}, s32[3,768]{1,0:T(4,128)}, u32[]{:S(2)}) copy-start(s32[3,768]{1,0:T(4,128)} %param.13) | copy-start | bytes 27652
  32.4 15.2 %all-to-all-start.1 = ((bf16[64,16,128]{2,1,0:T(8,128)(2,1)}), bf16[64,16,128]{2,1,0:T(8,128)(2,1)S(1)}, u32[]{:S(2)}, u32[]{:S(2)}) async-start(bf16[64,16,128]{2,1,0:T(8,128)(2,1)} %bitcast.5), calls=%async_computation.1 | async-start | bytes 524288 | tf_op jit(solution)/shard_map/all_to_all | solution.py:56
  41.1 8.6 %collective-permute-start.1 = (bf16[256,512]{1,0:T(8,128)(2,1)S(1)}, bf16[256,512]{1,0:T(8,128)(2,1)S(1)}, u32[]{:S(2)}, u32[]{:S(2)}) collective-permute-start(bf16[256,512]{1,0:T(8,128)(2,1)S(1)} %get-tuple-element.46), channel_id=1, source_target_pairs={{252,0},{0,4},{4,8},{8,12},{12,16},{16,20},{20,24},{24,28},{28,32}... | collective-permute-start | bytes 786440 | tf_op jit(solution)/shard_map/ppermute | solution.py:61
  49.7 41.2 %copy-start.22 = (f32[256]{0:T(256)S(1)}, f32[256]{0:T(256)}, u32[]{:S(2)}) copy-start(f32[256]{0:T(256)} %param.9) | copy-start | bytes 3076
  50.4 0.8 copy-start.3
  51.2 48.2 %copy-start = (f32[256,512]{1,0:T(8,128)S(1)}, f32[256,512]{1,0:T(8,128)}, u32[]{:S(2)}) copy-start(f32[256,512]{1,0:T(8,128)} %ent_ref.1) | copy-start | bytes 1572868
  62.7 23.8 %all-to-all-start.3 = ((bf16[256,4,128]{2,1,0:T(4,128)(2,1)}), bf16[256,4,128]{2,1,0:T(4,128)(2,1)S(1)}, u32[]{:S(2)}, u32[]{:S(2)}) async-start(bf16[256,4,128]{2,1,0:T(4,128)(2,1)} %bitcast.7), calls=%async_computation.3 | async-start | bytes 524288 | tf_op jit(solution)/shard_map/all_to_all | solution.py:56
  87.5 11.9 %all-to-all-start.4 = ((bf16[4,256,128]{2,1,0:T(8,128)(2,1)}), bf16[4,256,128]{2,1,0:T(8,128)(2,1)S(1)}, u32[]{:S(2)}, u32[]{:S(2)}) async-start(bf16[4,256,128]{2,1,0:T(8,128)(2,1)} %shard_map.115), calls=%async_computation.4 | async-start | bytes 524288 | tf_op jit(solution)/shard_map/all_to_all | solution.py:56
  100.8 9.7 %copy-start.14 = (f32[256,1]{1,0:T(8,128)}, f32[256,1]{1,0:T(8,128)S(1)}, u32[]{:S(2)}) copy-start(f32[256,1]{1,0:T(8,128)S(1)} %get-tuple-element.60.acc_ref) | copy-start | bytes 3076
  100.8 9.6 %collective-permute-start.2 = (bf16[256,512]{1,0:T(8,128)(2,1)S(1)}, bf16[256,512]{1,0:T(8,128)(2,1)S(1)}, u32[]{:S(2)}, u32[]{:S(2)}) collective-permute-start(bf16[256,512]{1,0:T(8,128)(2,1)S(1)} %get-tuple-element.49.ent_ref.refs_0_), channel_id=1, source_target_pairs={{8,0},{12,4},{16,8},{20,12},{24,16},{28,20},{32,24},{36,28},{40,32... | collective-permute-start | bytes 786440 | tf_op jit(solution)/shard_map/ppermute | solution.py:61
  104.7 15.7 %all-to-all-start.5 = ((bf16[64,16,128]{2,1,0:T(8,128)(2,1)}), bf16[64,16,128]{2,1,0:T(8,128)(2,1)S(1)}, u32[]{:S(2)}, u32[]{:S(2)}) async-start(bf16[64,16,128]{2,1,0:T(8,128)(2,1)} %bitcast.13), calls=%async_computation.5 | async-start | bytes 524288 | tf_op jit(solution)/shard_map/all_to_all | solution.py:56
  112.7 0.7 copy-start.10
  113.4 11.8 %collective-permute-start.3 = (bf16[256,512]{1,0:T(8,128)(2,1)}, bf16[256,512]{1,0:T(8,128)(2,1)}, u32[]{:S(2)}, u32[]{:S(2)}) collective-permute-start(bf16[256,512]{1,0:T(8,128)(2,1)} %get-tuple-element.56), channel_id=1, source_target_pairs={{248,0},{252,4},{0,8},{4,12},{8,16},{12,20},{16,24},{20,28},{24,32... | collective-permute-start | bytes 786440 | tf_op jit(solution)/shard_map/ppermute | solution.py:61
  120.4 1.0 copy-start.11
  122.7 16.5 %copy-start.9 = (bf16[1024,128]{1,0:T(8,128)(2,1)}, bf16[1024,128]{1,0:T(8,128)(2,1)S(1)}, u32[]{:S(2)}) copy-start(bf16[1024,128]{1,0:T(8,128)(2,1)S(1)} %get-tuple-element.58) | copy-start | bytes 786436
  139.2 23.2 %all-to-all-start.7 = ((bf16[256,4,128]{2,1,0:T(4,128)(2,1)}), bf16[256,4,128]{2,1,0:T(4,128)(2,1)S(1)}, u32[]{:S(2)}, u32[]{:S(2)}) async-start(bf16[256,4,128]{2,1,0:T(4,128)(2,1)} %bitcast.52), calls=%async_computation.7 | async-start | bytes 524288 | tf_op jit(solution)/shard_map/all_to_all | solution.py:56
  163.4 11.9 %all-to-all-start.8 = ((bf16[4,256,128]{2,1,0:T(8,128)(2,1)}), bf16[4,256,128]{2,1,0:T(8,128)(2,1)S(1)}, u32[]{:S(2)}, u32[]{:S(2)}) async-start(bf16[4,256,128]{2,1,0:T(8,128)(2,1)} %shard_map.120), calls=%async_computation.8 | async-start | bytes 524288 | tf_op jit(solution)/shard_map/all_to_all | solution.py:56
  175.3 0.9 copy-start.15
  177.0 0.8 copy-start.1
  177.8 5.0 %copy-start.8 = (bf16[1024,128]{1,0:T(8,128)(2,1)}, bf16[1024,128]{1,0:T(8,128)(2,1)S(1)}, u32[]{:S(2)}) copy-start(bf16[1024,128]{1,0:T(8,128)(2,1)S(1)} %get-tuple-element.63) | copy-start | bytes 786436
  177.8 11.2 %collective-permute-start.4 = (bf16[256,512]{1,0:T(8,128)(2,1)S(1)}, bf16[256,512]{1,0:T(8,128)(2,1)S(1)}, u32[]{:S(2)}, u32[]{:S(2)}) collective-permute-start(bf16[256,512]{1,0:T(8,128)(2,1)S(1)} %get-tuple-element.61.ent_ref.refs_0_), channel_id=1, source_target_pairs={{12,0},{16,4},{20,8},{24,12},{28,16},{32,20},{36,24},{40,28},{44,3... | collective-permute-start | bytes 786440 | tf_op jit(solution)/shard_map/ppermute | solution.py:61
  182.8 13.4 %all-to-all-start.9 = ((bf16[64,16,128]{2,1,0:T(8,128)(2,1)}), bf16[64,16,128]{2,1,0:T(8,128)(2,1)S(1)}, u32[]{:S(2)}, u32[]{:S(2)}) async-start(bf16[64,16,128]{2,1,0:T(8,128)(2,1)} %bitcast.51), calls=%async_computation.9 | async-start | bytes 524288 | tf_op jit(solution)/shard_map/all_to_all | solution.py:56
  191.2 0.7 copy-start.5
  191.9 0.7 copy-start.12
  192.6 12.8 %collective-permute-start.5 = (bf16[256,512]{1,0:T(8,128)(2,1)}, bf16[256,512]{1,0:T(8,128)(2,1)}, u32[]{:S(2)}, u32[]{:S(2)}) collective-permute-start(bf16[256,512]{1,0:T(8,128)(2,1)} %get-tuple-element.68), channel_id=1, source_target_pairs={{244,0},{248,4},{252,8},{0,12},{4,16},{8,20},{12,24},{16,28},{20,3... | collective-permute-start | bytes 786440 | tf_op jit(solution)/shard_map/ppermute | solution.py:61
  196.2 1.0 copy-start.13
  198.5 22.8 %copy-start.7 = (bf16[1024,128]{1,0:T(8,128)(2,1)}, bf16[1024,128]{1,0:T(8,128)(2,1)S(1)}, u32[]{:S(2)}) copy-start(bf16[1024,128]{1,0:T(8,128)(2,1)S(1)} %get-tuple-element.70) | copy-start | bytes 786436
  205.4 1.0 copy-start.6
  221.3 21.3 %all-to-all-start.11 = ((bf16[256,4,128]{2,1,0:T(4,128)(2,1)}), bf16[256,4,128]{2,1,0:T(4,128)(2,1)S(1)}, u32[]{:S(2)}, u32[]{:S(2)}) async-start(bf16[256,4,128]{2,1,0:T(4,128)(2,1)} %bitcast.50), calls=%async_computation.11 | async-start | bytes 524288 | tf_op jit(solution)/shard_map/all_to_all | solution.py:56
  227.0 1.0 copy-start.4
  229.0 18.8 %copy-start.18 = (s32[1,4,64,4]{2,1,3,0:T(4,128)S(1)}, s32[1,4,64,4]{2,1,3,0:T(4,128)}, u32[]{:S(2)}) copy-start(s32[1,4,64,4]{2,1,3,0:T(4,128)} %get-tuple-element.82) | copy-start | bytes 12292
  242.6 23.2 %all-to-all-start.13 = ((bf16[64,16,512]{2,1,0:T(8,128)(2,1)}), bf16[64,16,512]{2,1,0:T(8,128)(2,1)S(1)}, u32[]{:S(2)}, u32[]{:S(2)}) async-start(bf16[64,16,512]{2,1,0:T(8,128)(2,1)} %bitcast.22), calls=%async_computation.13 | async-start | bytes 2097152 | tf_op jit(solution)/shard_map/all_to_all | solution.py:56
  265.7 13.3 %all-to-all-start.12 = ((bf16[4,256,128]{2,1,0:T(8,128)(2,1)}), bf16[4,256,128]{2,1,0:T(8,128)(2,1)S(1)}, u32[]{:S(2)}, u32[]{:S(2)}) async-start(bf16[4,256,128]{2,1,0:T(8,128)(2,1)} %shard_map.125), calls=%async_computation.12 | async-start | bytes 524288 | tf_op jit(solution)/shard_map/all_to_all | solution.py:56
  269.2 15.8 %copy-start.2 = (f32[256,512]{1,0:T(8,128)S(1)}, f32[256,512]{1,0:T(8,128)}, u32[]{:S(2)}) copy-start(f32[256,512]{1,0:T(8,128)} %copy-done.1) | copy-start | bytes 1572868
  279.0 23.9 %all-to-all-start.14 = ((bf16[64,16,512]{2,1,0:T(8,128)(2,1)}), bf16[64,16,512]{2,1,0:T(8,128)(2,1)S(1)}, u32[]{:S(2)}, u32[]{:S(2)}) async-start(bf16[64,16,512]{2,1,0:T(8,128)(2,1)} %shard_map.130), calls=%async_computation.14 | async-start | bytes 2097152 | tf_op jit(solution)/shard_map/all_to_all | solution.py:56
  286.8 16.6 %copy-start.16 = (f32[2,512,512]{2,1,0:T(8,128)S(1)}, f32[2,512,512]{2,1,0:T(8,128)}, u32[]{:S(2)}) copy-start(f32[2,512,512]{2,1,0:T(8,128)} %param.10) | copy-start | bytes 6291460
  302.9 1.6 copy-start.17
